TPU v7x, 32 devices: a whole 2x2x4 slice. The times are simulated.
32 devices in a mesh: dp: 8 (over z, x), tensor: 4 (over y, core).
Axes of the slice: x: 2, y: 2, z: 4, core: 2. Of those that a mesh axis runs over, the one named last changes fastest.
Arguments:
- patches: bfloat16 [24, 2048, 1024], P('dp', 'tensor'), may hold values from -6 to 6
- cotangent: bfloat16 [24, 2048, 1024], P('dp', 'tensor'), may hold values from -6 to 6
- empty_slots: int32 [8], replicated, may hold values from 0 to 2
- dataset_id: int32 [24], replicated, may hold values from 0 to 5
- dataset_weight: int32 [6], replicated, may hold values from 1 to 8
- query_key_value_weight: bfloat16 [3, 1024, 1024], P(None, None, 'tensor'), may hold values from -0.25 to 0.25
- qv_bias: float32 [2, 1024], P(None, 'tensor'), may hold values from -3 to 3
- output_projection_weight: bfloat16 [1024, 1024], P('tensor'), may hold values from -0.75 to 0.75
- out_bias: float32 [1024], replicated, may hold values from -2 to 2
- up_projection_weight: bfloat16 [1024, 4096], P(None, 'tensor'), may hold values from -0.1875 to 0.1875
- up_bias: float32 [4096], P('tensor'), may hold values from -2 to 2
- down_projection_weight: bfloat16 [4096, 1024], P('tensor'), may hold values from -0.09375 to 0.09375
- down_bias: float32 [1024], replicated, may hold values from -2 to 2
- attn_gain: float32 [1024], replicated, may hold values from 0.5 to 1.5
- attn_shift: float32 [1024], replicated, may hold values from -1.5 to 1.5
- mlp_gain: float32 [1024], replicated, may hold values from 0.5 to 1.5
- mlp_shift: float32 [1024], replicated, may hold values from -1.5 to 1.5
Outputs:
- block_out: bfloat16 [24, 2048, 1024], P('dp', 'tensor')
- grad_patches: bfloat16 [24, 2048, 1024], P('dp', 'tensor')
- grad_qkv_weight: float32 [3, 1024, 1024], P(None, None, 'tensor')
- grad_qv_bias: float32 [2, 1024], P(None, 'tensor')
- grad_out_weight: float32 [1024, 1024], P('tensor')
- grad_out_bias: float32 [1024], replicated
- grad_up_weight: float32 [1024, 4096], P(None, 'tensor')
- grad_up_bias: float32 [4096], P('tensor')
- grad_down_weight: float32 [4096, 1024], P('tensor')
- grad_down_bias: float32 [1024], replicated
- grad_attn_gain: float32 [1024], replicated
- grad_attn_shift: float32 [1024], replicated
- sensitivity_feedforward_scale: float32 [1024], replicated
- grad_mlp_shift: float32 [1024], replicated
All inputs are finite; a program needn't handle non-finite values.
Results may differ from a plain program's by a relative error of at most 0.02.
Values may be sent and summed in bfloat16 or wider, within the bound.
No kernel may reach another device: no remote copies, remote signals or barrier semaphores. Data moves between devices by JAX's collectives and lax.ppermute only.
A program may use at most 256 MiB of HBM per device.

v0:
```python
import jax
import jax.numpy as jnp
from jax import lax
from jax.sharding import PartitionSpec as P

HD = 64
epsilon = 1e-05


def norm_rows(source, norm_gain, norm_shift):
    row_mean = jnp.mean(source, axis=-1, keepdims=True)
    centred = source - row_mean
    spread = jnp.mean(centred * centred, axis=-1, keepdims=True)
    return centred * lax.rsqrt(spread + epsilon) * norm_gain + norm_shift


def gelu_exact(pre_act):
    return jax.nn.gelu(pre_act, approximate=False)


def split_heads(array, head_count):
    return array.reshape(array.shape[0], array.shape[1], head_count, HD)


def attend_item(operands):
    queries, key_rows, values = operands
    length, head_count, head_size = queries.shape
    qblock = min(512, length)
    score_scale = head_size ** (-0.5)
    blocks = queries.reshape(length // qblock, qblock, head_count, head_size)

    def one_block(query_block):
        scores = (
            jnp.einsum("qhd,khd->hqk", query_block, key_rows, preferred_element_type=jnp.float32)
            * score_scale
        )
        row_top = jnp.max(scores, axis=-1, keepdims=True)
        exp_scores = jnp.exp(scores - row_top)
        row_total = jnp.sum(exp_scores, axis=-1, keepdims=True)
        attn_weights = (exp_scores / row_total).astype(jnp.bfloat16)
        attended = jnp.einsum(
            "hqk,khd->qhd", attn_weights, values, preferred_element_type=jnp.float32
        )
        return (attended.astype(jnp.bfloat16), (row_top + jnp.log(row_total))[:, :, 0])

    attended, log_total = lax.map(one_block, blocks)
    return (attended.reshape(length, head_count, head_size), log_total)


def attend_back(operands):
    queries, key_rows, values, grad_attended, log_total = operands
    length, head_count, head_size = queries.shape
    qblock = min(512, length)
    score_scale = head_size ** (-0.5)
    query_blocks = queries.reshape(length // qblock, qblock, head_count, head_size)
    grad_blocks = grad_attended.reshape(length // qblock, qblock, head_count, head_size)

    def one_block(carried, block_in):
        query_block, grad_block, lse_block = block_in
        scores = (
            jnp.einsum("qhd,khd->hqk", query_block, key_rows, preferred_element_type=jnp.float32)
            * score_scale
        )
        attn_weights = jnp.exp(scores - lse_block[:, :, None])
        grad_weights = jnp.einsum(
            "qhd,khd->hqk", grad_block, values, preferred_element_type=jnp.float32
        )
        grad_scores = attn_weights * (
            grad_weights - jnp.sum(attn_weights * grad_weights, axis=-1, keepdims=True)
        )
        grad_low = grad_scores.astype(jnp.bfloat16)
        sensitivity_questions = (
            jnp.einsum("hqk,khd->qhd", grad_low, key_rows, preferred_element_type=jnp.float32)
            * score_scale
        )
        key_acc = (
            carried[0]
            + jnp.einsum("hqk,qhd->khd", grad_low, query_block, preferred_element_type=jnp.float32)
            * score_scale
        )
        value_acc = carried[1] + jnp.einsum(
            "hqk,qhd->khd",
            attn_weights.astype(jnp.bfloat16),
            grad_block,
            preferred_element_type=jnp.float32,
        )
        return ((key_acc, value_acc), sensitivity_questions)

    zero_acc = jnp.zeros((length, head_count, head_size), jnp.float32)
    (grad_keys, grad_values), grad_queries = lax.scan(
        one_block, (zero_acc, zero_acc), (query_blocks, grad_blocks, log_total)
    )
    return (grad_queries.reshape(length, head_count, head_size), grad_keys, grad_values)


def shards(
    patches,
    cotangent,
    empty_slots,
    dataset_id,
    dataset_weight,
    query_key_value_weight,
    qv_bias,
    output_projection_weight,
    out_bias,
    up_projection_weight,
    up_bias,
    down_projection_weight,
    down_bias,
    attn_gain,
    attn_shift,
    mlp_gain,
    mlp_shift,
):
    number_format = jnp.float32
    half_type = jnp.bfloat16
    slot_count = patches.shape[0]
    group_slots = empty_slots.shape[0]
    slot_index = jnp.arange(group_slots * slot_count, dtype=jnp.int32) % slot_count
    filled = jnp.repeat(slot_count - empty_slots, slot_count)
    valid_all = (slot_index < filled).astype(number_format)
    table_hits = (
        dataset_id[:, None] == jnp.arange(dataset_weight.shape[0], dtype=jnp.int32)[None, :]
    )
    numerator = jnp.sum(jnp.where(table_hits, dataset_weight[None, :], 0), axis=1).astype(
        number_format
    )
    total_items = jnp.sum(valid_all)
    total_weight = jnp.sum(valid_all * numerator)
    multiplier_whole = valid_all * numerator * total_items / total_weight
    own_start = lax.axis_index("dp") * slot_count
    own_scale = lax.dynamic_slice_in_dim(multiplier_whole, own_start, slot_count)
    own_valid = lax.dynamic_slice_in_dim(valid_all, own_start, slot_count)
    inputs = patches.astype(number_format)
    normed = norm_rows(inputs, attn_gain, attn_shift).astype(half_type)
    normalized_every = lax.all_gather(normed, "tensor", axis=1, tiled=True)
    local_width = query_key_value_weight.shape[2]
    head_count = local_width // HD
    projected_rows = jnp.einsum(
        "owz,gzh->gowh",
        normalized_every,
        query_key_value_weight,
        preferred_element_type=number_format,
    )
    queries = split_heads((projected_rows[0] + qv_bias[0]).astype(half_type), head_count)
    key_rows = split_heads(projected_rows[1].astype(half_type), head_count)
    values = split_heads((projected_rows[2] + qv_bias[1]).astype(half_type), head_count)
    attended, log_total = lax.map(attend_item, (queries, key_rows, values))
    attended_matrix = attended.reshape(slot_count, attended.shape[1], local_width)
    attn_part = jnp.einsum(
        "ifz,zp->ifp",
        attended_matrix,
        output_projection_weight,
        preferred_element_type=number_format,
    )
    attn_rows = lax.psum_scatter(
        attn_part.astype(jnp.bfloat16), "tensor", scatter_dimension=1, tiled=True
    ).astype(jnp.float32)
    residual = inputs + attn_rows + out_bias
    normed_mlp = norm_rows(residual, mlp_gain, mlp_shift).astype(half_type)
    cot_scaled = cotangent.astype(number_format) * own_scale[:, None, None]
    cot_low = cot_scaled.astype(half_type)
    normalized_perceptron_every = lax.all_gather(normed_mlp, "tensor", axis=1, tiled=True)
    hidden_pre = (
        jnp.einsum(
            "jzb,bu->jzu",
            normalized_perceptron_every,
            up_projection_weight,
            preferred_element_type=number_format,
        )
        + up_bias
    )
    gelu_out, gelu_back = jax.vjp(gelu_exact, hidden_pre)
    latent_activations = gelu_out.astype(half_type)
    perceptron_portion = jnp.einsum(
        "vuc,cy->vuy",
        latent_activations,
        down_projection_weight,
        preferred_element_type=number_format,
    )
    mlp_rows = lax.psum_scatter(
        perceptron_portion.astype(jnp.bfloat16), "tensor", scatter_dimension=1, tiled=True
    ).astype(jnp.float32)
    output = ((residual + mlp_rows + down_bias) * own_valid[:, None, None]).astype(half_type)
    adjoint_for_each_layer = lax.all_gather(cot_low, "tensor", axis=1, tiled=True)
    hidden_gradient = jnp.einsum(
        "eph,wh->epw",
        adjoint_for_each_layer,
        down_projection_weight,
        preferred_element_type=number_format,
    )
    preactivation_gradient = gelu_back(hidden_gradient)[0].astype(half_type)
    down_gradient = jnp.einsum(
        "wuf,wul->fl",
        latent_activations,
        adjoint_for_each_layer,
        preferred_element_type=number_format,
    )
    up_gradient = jnp.einsum(
        "eug,eut->gt",
        normalized_perceptron_every,
        preactivation_gradient,
        preferred_element_type=number_format,
    )
    grad_up_bias = jnp.sum(preactivation_gradient.astype(number_format), axis=(0, 1))
    norm_portion = jnp.einsum(
        "jmn,hn->jmh",
        preactivation_gradient,
        up_projection_weight,
        preferred_element_type=number_format,
    )
    grad_normed_mlp = lax.psum_scatter(
        norm_portion.astype(jnp.bfloat16), "tensor", scatter_dimension=1, tiled=True
    ).astype(jnp.float32)
    mlp_norm_back = jax.vjp(norm_rows, residual, mlp_gain, mlp_shift)[1]
    grad_resid_norm, sensitivity_feedforward_scale, grad_mlp_shift = mlp_norm_back(grad_normed_mlp)
    grad_residual = cot_scaled + grad_resid_norm
    grad_out_bias = jnp.sum(grad_residual, axis=(0, 1))
    grad_down_bias = jnp.sum(cot_scaled, axis=(0, 1))
    residual_gradient_every = lax.all_gather(
        grad_residual.astype(half_type), "tensor", axis=1, tiled=True
    )
    grad_attended = jnp.einsum(
        "xmn,wn->xmw",
        residual_gradient_every,
        output_projection_weight,
        preferred_element_type=number_format,
    ).astype(half_type)
    grad_out = jnp.einsum(
        "ift,ifr->tr",
        attended_matrix,
        residual_gradient_every,
        preferred_element_type=number_format,
    )
    grad_queries, grad_keys, grad_values = lax.map(
        attend_back, (queries, key_rows, values, split_heads(grad_attended, head_count), log_total)
    )
    flat_shape = (slot_count, grad_queries.shape[1], local_width)
    projection_gradient = jnp.stack(
        [
            grad_queries.reshape(flat_shape).astype(half_type),
            grad_keys.reshape(flat_shape).astype(half_type),
            grad_values.reshape(flat_shape).astype(half_type),
        ]
    )
    query_key_value_gradient = jnp.einsum(
        "ktr,jktq->jrq", normalized_every, projection_gradient, preferred_element_type=number_format
    )
    grad_qv = jnp.stack(
        [
            jnp.sum(projection_gradient[0].astype(number_format), axis=(0, 1)),
            jnp.sum(projection_gradient[2].astype(number_format), axis=(0, 1)),
        ]
    )
    normed_part = jnp.einsum(
        "vbmk,vxk->bmx",
        projection_gradient,
        query_key_value_weight,
        preferred_element_type=number_format,
    )
    grad_normed = lax.psum_scatter(
        normed_part.astype(jnp.bfloat16), "tensor", scatter_dimension=1, tiled=True
    ).astype(jnp.float32)
    attn_norm_back = jax.vjp(norm_rows, inputs, attn_gain, attn_shift)[1]
    grad_input_norm, grad_attn_gain, grad_attn_shift = attn_norm_back(grad_normed)
    grad_inputs = (grad_residual + grad_input_norm).astype(half_type)
    summed = (
        lax.psum(query_key_value_gradient.astype(jnp.bfloat16), "dp").astype(jnp.float32),
        lax.psum(grad_qv.astype(jnp.bfloat16), "dp").astype(jnp.float32),
        lax.psum(grad_out.astype(jnp.bfloat16), "dp").astype(jnp.float32),
        lax.psum(up_gradient.astype(jnp.bfloat16), "dp").astype(jnp.float32),
        lax.psum(grad_up_bias.astype(jnp.bfloat16), "dp").astype(jnp.float32),
        lax.psum(down_gradient.astype(jnp.bfloat16), "dp").astype(jnp.float32),
    )
    small_sums = lax.psum(
        (
            grad_attn_gain,
            grad_attn_shift,
            sensitivity_feedforward_scale,
            grad_mlp_shift,
            grad_out_bias,
            grad_down_bias,
        ),
        ("dp", "tensor"),
    )
    return (
        output,
        grad_inputs,
        summed[0] / total_items,
        summed[1] / total_items,
        summed[2] / total_items,
        small_sums[4] / total_items,
        summed[3] / total_items,
        summed[4] / total_items,
        summed[5] / total_items,
        small_sums[5] / total_items,
        small_sums[0] / total_items,
        small_sums[1] / total_items,
        small_sums[2] / total_items,
        small_sums[3] / total_items,
    )


def solution(mesh):
    placed = (
        P("dp", "tensor", None),
        P("dp", "tensor", None),
        P(),
        P(),
        P(),
        P(None, None, "tensor"),
        P(None, "tensor"),
        P("tensor", None),
        P(),
        P(None, "tensor"),
        P("tensor"),
        P("tensor", None),
        P(),
        P(),
        P(),
        P(),
        P(),
    )
    return jax.shard_map(
        shards,
        mesh=mesh,
        in_specs=placed,
        out_specs=(
            P("dp", "tensor", None),
            P("dp", "tensor", None),
            P(None, None, "tensor"),
            P(None, "tensor"),
            P("tensor", None),
            P(),
            P(None, "tensor"),
            P("tensor"),
            P("tensor", None),
            P(),
            P(),
            P(),
            P(),
            P(),
        ),
        check_vma=False,
    )
```

profile of v0, /device:TPU:0, one launch (start us, length us, event | category | flops | bytes accessed | tf_op | source)
XLA Modules:
  0.0 1974.1 jit_solution(18060391247935320922)
XLA Ops:
  16.7 84.7 %all-gather.5.cloned.1.call-done = bf16[3,2048,1024]{2,1,0:T(8,128)(2,1)} async-done(((bf16[3,512,1024]{2,1,0:T(8,128)(2,1)}), bf16[3,2048,1024]{2,1,0:T(8,128)(2,1)}) %all-gather.5.cloned.1.call-update) | async-done | bytes 12582928 | tf_op jit(solution)/shard_map/all_gather | solution.py:136
  101.4 17.1 fusion.58
  123.4 11.4 fusion.102
  144.1 192.9 %while.54 = (s32[]{:T(128)}, bf16[3,2048,4,64]{1,3,2,0:T(8,128)(2,1)}, f32[3,4,4,512]{3,2,1,0:T(4,128)}, bf16[3,2048,4,64]{1,3,2,0:T(8,128)(2,1)}, bf16[3,2048,4...) while((s32[]{:T(128)}, ...), condition=%wide.region_7.8_spmd, body=%wide.region_2.7_spmd.sunk | while | flops 1111619584 | bytes 74055984 | solution.py:148
  152.4 47.4 %while.57 = (s32[]{:T(128)}, bf16[4,512,4,64]{1,3,2,0:T(8,128)(2,1)}, f32[4,4,512]{2,1,0:T(4,128)S(1)}, bf16[4,512,4,64]{1,3,2,0:T(8,128)(2,1)}, bf16[2048,4,64]...) while((s32[]{:T(128)}, bf16[4,512,4,64]{1,3,2,0:T(8,128)(2,1)}, ...), condition=%wide.region_6.6_spmd, body=%wide.region_3.5_spmd.sunk | while | flops 1111619584 | bytes 57213052 | solution.py:46
  216.6 47.4 %while.57 = (s32[]{:T(128)}, bf16[4,512,4,64]{1,3,2,0:T(8,128)(2,1)}, f32[4,4,512]{2,1,0:T(4,128)S(1)}, bf16[4,512,4,64]{1,3,2,0:T(8,128)(2,1)}, bf16[2048,4,64]...) while((s32[]{:T(128)}, bf16[4,512,4,64]{1,3,2,0:T(8,128)(2,1)}, ...), condition=%wide.region_6.6_spmd, body=%wide.region_3.5_spmd.sunk | while | flops 1111619584 | bytes 57213052 | solution.py:46
  280.8 47.4 %while.57 = (s32[]{:T(128)}, bf16[4,512,4,64]{1,3,2,0:T(8,128)(2,1)}, f32[4,4,512]{2,1,0:T(4,128)S(1)}, bf16[4,512,4,64]{1,3,2,0:T(8,128)(2,1)}, bf16[2048,4,64]...) while((s32[]{:T(128)}, bf16[4,512,4,64]{1,3,2,0:T(8,128)(2,1)}, ...), condition=%wide.region_6.6_spmd, body=%wide.region_3.5_spmd.sunk | while | flops 1111619584 | bytes 57213052 | solution.py:46
  336.9 10.1 convolution_convert_fusion.2
  347.1 99.1 %reduce-scatter.5.cloned.1.call-done = bf16[3,512,1024]{2,1,0:T(8,128)(2,1)} async-done(((bf16[3,2048,1024]{2,1,0:T(8,128)(2,1)}), bf16[3,512,1024]{2,1,0:T(8,128)(2,1)}) %reduce-scatter.5.cloned.1.call-update) | async-done | bytes 3145744 | tf_op jit(solution)/shard_map/reduce_scatter | solution.py:156
  465.1 73.9 %all-gather.7.cloned.1.call-done = bf16[3,2048,1024]{2,1,0:T(8,128)(2,1)} async-done(((bf16[3,512,1024]{2,1,0:T(8,128)(2,1)}), bf16[3,2048,1024]{2,1,0:T(8,128)(2,1)}) %all-gather.7.cloned.1.call-update) | async-done | bytes 12582928 | tf_op jit(solution)/shard_map/all_gather | solution.py:163
  539.1 29.6 %fusion.72 = (u8[2048,1024]{1,0:T(8,128)(4,1)}, u8[2048,1024]{1,0:T(8,128)(4,1)}, f32[3,2048,1024]{2,1,0:T(8,128)}) fusion(f32[1024]{0:T(1024)S(1)} %copy-done.41, bf16[3,2048,1024]{2,1,0:T(8,128)(2,1)} %all-gather.7.cloned.1.call-done, bf16[1024,1024]{1,0:T(8,128)(2,1)S(1)} %copy-done), kind=kOutput, calls=%fused_computation.128 | convolution fusion | flops 12968787968 | bytes 44044288 | tf_op jit(solution)/shard_map/jzb,bu->jzu/dot_general | solution.py:165
  568.7 61.6 %multiply_convert_fusion.1 = (bf16[3,2048,1024]{2,1,0:T(8,128)(2,1)}, f32[3,2048,1024]{2,1,0:T(8,128)}) fusion(f32[3,2048,1024]{2,1,0:T(8,128)} %get-tuple-element.412, f32[1024]{0:T(1024)S(1)} %copy-done.41, u8[2048,1024]{1,0:T(8,128)(4,1)} %get-tuple-element.313, u8[2048,1024]{1,0:T(8,128)(4,1)} %get-tuple-element.312), kind=kLoop, calls=%fused_computation.67 | loop fusion | flops 446693376 | bytes 67112960 | tf_op jit(solution)/shard_map/convert_element_type | solution.py:174
  630.3 32.6 %fusion.103 = (bf16[1024]{0:T(1024)(128)(2,1)}, bf16[3,2048,1024]{2,1,0:T(8,128)(2,1)}) fusion(f32[3,2048,1024]{2,1,0:T(8,128)} %get-tuple-element.399, bf16[3,2048,1024]{2,1,0:T(8,128)(2,1)} %all-gather.9.cloned.1.call-done, bf16[1024,1024]{1,0:T(8,128)(2,1)} %param.36, f32[3,2048,1024]{2,1,0:T(8,128)} %get-tuple-element.412, f32[1024]{0:T(1024)S(1)} %copy-done.41), kind=kOutput, calls=%fused_computation.192 | convolution fusion | flops 12985564160 | bytes 77600768 | tf_op jit(solution)/shard_map/eph,wh->epw/dot_general | solution.py:186
  662.9 20.4 %convolution_convert_fusion = bf16[3,2048,1024]{2,1,0:T(8,128)(2,1)} fusion(bf16[3,2048,1024]{2,1,0:T(8,128)(2,1)} %get-tuple-element.414, bf16[1024,1024]{1,0:T(8,128)(2,1)S(1)} %copy-done), kind=kOutput, calls=%fused_computation.105 | convolution fusion | flops 12891193344 | bytes 27262976 | tf_op jit(solution)/shard_map/jmn,hn->jmh/dot_general | solution.py:206
  684.8 21.3 %convolution_convert_fusion.1 = bf16[3,2048,1024]{2,1,0:T(8,128)(2,1)} fusion(bf16[3,2048,1024]{2,1,0:T(8,128)(2,1)} %get-tuple-element.398, bf16[1024,1024]{1,0:T(8,128)(2,1)S(1)} %copy-done.47), kind=kOutput, calls=%fused_computation.106 | convolution fusion | flops 12891193344 | bytes 27262976 | tf_op jit(solution)/shard_map/vuc,cy->vuy/dot_general | solution.py:175
  706.3 76.2 %reduce-scatter.9.cloned.1.call-done = bf16[3,512,1024]{2,1,0:T(8,128)(2,1)} async-done(((bf16[3,2048,1024]{2,1,0:T(8,128)(2,1)}), bf16[3,512,1024]{2,1,0:T(8,128)(2,1)}) %reduce-scatter.9.cloned.1.call-update) | async-done | bytes 3145744 | tf_op jit(solution)/shard_map/reduce_scatter | solution.py:212
  795.7 88.3 %reduce-scatter.7.cloned.1.call-done = bf16[3,512,1024]{2,1,0:T(8,128)(2,1)} async-done(((bf16[3,2048,1024]{2,1,0:T(8,128)(2,1)}), bf16[3,512,1024]{2,1,0:T(8,128)(2,1)}) %reduce-scatter.7.cloned.1.call-update) | async-done | bytes 3145744 | tf_op jit(solution)/shard_map/reduce_scatter | solution.py:181
  884.0 10.3 fusion.100
  899.3 19.5 bitcast_convert_fusion.1
  918.9 19.0 bitcast_convert_fusion.2
  937.8 43.7 %all-gather.11.cloned.1.call-done = bf16[3,2048,1024]{2,1,0:T(8,128)(2,1)} async-done(((bf16[3,512,1024]{2,1,0:T(8,128)(2,1)}), bf16[3,2048,1024]{2,1,0:T(8,128)(2,1)}) %all-gather.11.cloned.1.call-update) | async-done | bytes 12582928 | tf_op jit(solution)/shard_map/all_gather | solution.py:220
  981.5 14.3 convolution_convert_fusion.3
  995.9 553.7 %while.56 = (s32[]{:T(128)}, bf16[3,2048,4,64]{1,3,2,0:T(8,128)(2,1)}, bf16[3,2048,4,64]{1,3,2,0:T(8,128)(2,1)}, bf16[3,2048,4,64]{1,3,2,0:T(8,128)(2,1)}, bf16[...) while((s32[]{:T(128)}, ...), condition=%wide.region_22.23_spmd, body=%wide.region_18.22_spmd.sunk | while | flops 2737436672 | bytes 246014544 | solution.py:235
  1010.8 158.2 %while.58 = (s32[]{:T(128)}, f32[2048,4,64]{0,2,1:T(8,128)}, f32[2048,4,64]{0,2,1:T(8,128)}, bf16[4,512,4,64]{1,3,2,0:T(8,128)(2,1)}, bf16[4,512,4,64]{1,3,2,0:T...) while((s32[]{:T(128)}, f32[2048,4,64]{0,2,1:T(8,128)}, ...), condition=%wide.region_21.21_spmd.clone, body=%wide.region_19.20_spmd.clone.sunk | while | flops 2737436672 | bytes 206102832 | solution.py:90
  1028.9 10.6 multiply_convert_fusion.4
  1059.0 9.4 multiply_reduce_fusion.5
  1068.4 10.6 multiply_convert_fusion.4
  1098.6 9.4 multiply_reduce_fusion.5
  1108.0 10.6 multiply_convert_fusion.4
  1147.5 10.6 multiply_convert_fusion.4
  1195.3 158.2 %while.58 = (s32[]{:T(128)}, f32[2048,4,64]{0,2,1:T(8,128)}, f32[2048,4,64]{0,2,1:T(8,128)}, bf16[4,512,4,64]{1,3,2,0:T(8,128)(2,1)}, bf16[4,512,4,64]{1,3,2,0:T...) while((s32[]{:T(128)}, f32[2048,4,64]{0,2,1:T(8,128)}, ...), condition=%wide.region_21.21_spmd.clone, body=%wide.region_19.20_spmd.clone.sunk | while | flops 2737436672 | bytes 206102832 | solution.py:90
  1213.3 10.6 multiply_convert_fusion.4
  1243.4 9.4 multiply_reduce_fusion.5
  1252.9 10.6 multiply_convert_fusion.4
  1292.4 10.6 multiply_convert_fusion.4
  1332.0 10.6 multiply_convert_fusion.4
  1379.8 158.2 %while.58 = (s32[]{:T(128)}, f32[2048,4,64]{0,2,1:T(8,128)}, f32[2048,4,64]{0,2,1:T(8,128)}, bf16[4,512,4,64]{1,3,2,0:T(8,128)(2,1)}, bf16[4,512,4,64]{1,3,2,0:T...) while((s32[]{:T(128)}, f32[2048,4,64]{0,2,1:T(8,128)}, ...), condition=%wide.region_21.21_spmd.clone, body=%wide.region_19.20_spmd.clone.sunk | while | flops 2737436672 | bytes 206102832 | solution.py:90
  1397.8 10.6 multiply_convert_fusion.4
  1437.4 10.6 multiply_convert_fusion.4
  1476.9 10.6 multiply_convert_fusion.4
  1516.4 10.6 multiply_convert_fusion.4
  1563.5 9.9 fusion.89
  1573.3 13.9 fusion.86
  1588.6 15.4 bitcast_convert_fusion
  1609.1 22.8 %all-reduce.1 = (bf16[2,256]{1,0:T(2,128)(2,1)S(1)}, bf16[1024]{0:T(1024)(128)(2,1)S(1)}) all-reduce(bf16[2,256]{1,0:T(2,128)(2,1)S(1)} %pad_maximum_fusion.7, bf16[1024]{0:T(1024)(128)(2,1)S(1)} %copy-done.45), channel_id=1, replica_groups=mesh['dp'=8,'tensor'=4] {'dp'}, use_global_device_ids=true, to_apply=%region_29.30 | all-reduce | flops 1536 | bytes 6144 | tf_op jit(solution)/shard_map/psum | solution.py:269
  1634.4 167.8 %all-reduce.5.cloned.1.call-done = (bf16[3,1024,256]{1,2,0:T(8,128)(2,1)}, bf16[256,1024]{1,0:T(8,128)(2,1)}, bf16[1024,1024]{1,0:T(8,128)(2,1)}, bf16[1024,1024]{1,0:T(8,128)(2,1)}) async-done(((bf16[3,1024,256]{1,2,0:T(8,128)(2,1)}, bf16[256,1024]{1,0:T(8,128)(2,1)}, bf16[1024,1024]{1,0:T(8,128)(2,1)}, bf16[1024,1024]{1,0:T(8,128)(2,1)}), (bf16[3,1024,256]{1,2,0:T(8,128)(2,1)}, ...) | async-done | bytes 6291472 | tf_op jit(solution)/shard_map/psum | solution.py:268
  1821.7 81.2 %reduce-scatter.11.cloned.1.call-done = bf16[3,512,1024]{2,1,0:T(8,128)(2,1)} async-done(((bf16[3,2048,1024]{2,1,0:T(8,128)(2,1)}), bf16[3,512,1024]{2,1,0:T(8,128)(2,1)}) %reduce-scatter.11.cloned.1.call-update) | async-done | bytes 3145744 | tf_op jit(solution)/shard_map/reduce_scatter | solution.py:261
  1912.9 39.7 %all-reduce = (f32[1024]{0:T(1024)S(1)}, f32[1024]{0:T(1024)S(1)}, f32[1024]{0:T(1024)S(1)}, f32[1024]{0:T(1024)S(1)}, f32[1024]{0:T(1024)S(1)}, /*index=5*/f32[1024]{0:T(1024)S(1)}) all-reduce(f32[1024]{0:T(1024)S(1)} %copy-done.37, f32[1024]{0:T(1024)S(1)} %copy-done.38, ...), channel_id=1, replica_groups=mesh['dp'=8,'tensor'=4] {'dp','tensor'}, use_global_device_ids=true, to_apply=%region_32.33 | all-reduce | flops 6144 | bytes 49152 | tf_op jit(solution)/shard_map/psum | solution.py:275
  (518 shorter events, 718.9 us)
Async XLA Ops:
  7.2 531.9 %copy-start = (bf16[1024,1024]{1,0:T(8,128)(2,1)S(1)}, bf16[1024,1024]{1,0:T(8,128)(2,1)}, u32[]{:S(2)}) copy-start(bf16[1024,1024]{1,0:T(8,128)(2,1)} %param.34) | copy-start | bytes 6291460
  7.2 94.1 %all-gather.5.cloned.1.call-start = ((), (), s32[]{:S(2)}) async-start(), calls=%async_computation.4 | async-start | bytes 15728640 | tf_op jit(solution)/shard_map/all_gather | solution.py:136
  16.4 429.9 %reduce-scatter.5.cloned.1.call-start = ((), (), s32[]{:S(2)}) async-start(), calls=%async_computation.5 | async-start | bytes 15728640 | tf_op jit(solution)/shard_map/reduce_scatter | solution.py:156
  347.0 99.2 %copy-start.23 = (f32[1024]{0:T(1024)S(1)}, f32[1024]{0:T(1024)}, u32[]{:S(2)}) copy-start(f32[1024]{0:T(1024)} %param.33) | copy-start | bytes 12292
  347.1 106.7 %copy-start.32 = (f32[1024]{0:T(1024)S(1)}, f32[1024]{0:T(1024)}, u32[]{:S(2)}) copy-start(f32[1024]{0:T(1024)} %param.40) | copy-start | bytes 12292
  347.1 106.7 %copy-start.39 = (f32[1024]{0:T(1024)S(1)}, f32[1024]{0:T(1024)}, u32[]{:S(2)}) copy-start(f32[1024]{0:T(1024)} %param.41) | copy-start | bytes 12292
  347.1 192.0 %all-gather.7.cloned.1.call-start = ((), (), s32[]{:S(2)}) async-start(), calls=%async_computation.6 | async-start | bytes 15728640 | tf_op jit(solution)/shard_map/all_gather | solution.py:163
  456.8 82.3 %copy-start.41 = (f32[1024]{0:T(1024)S(1)}, f32[1024]{0:T(1024)}, u32[]{:S(2)}) copy-start(f32[1024]{0:T(1024)} %param.35) | copy-start | bytes 12292
  456.8 173.5 %all-gather.9.cloned.1.call-start = ((), (), s32[]{:S(2)}) async-start(), calls=%async_computation.8 | async-start | bytes 15728640 | tf_op jit(solution)/shard_map/all_gather | solution.py:185
  460.3 108.4 %copy-start.43 = (f32[3]{0:T(128)}, f32[3]{0:T(128)S(1)}, u32[]{:S(2)}) copy-start(f32[3]{0:T(128)S(1)} %dynamic_slice.47) | copy-start | bytes 40
  465.1 317.4 %reduce-scatter.9.cloned.1.call-start = ((), (), s32[]{:S(2)}) async-start(), calls=%async_computation.9 | async-start | bytes 15728640 | tf_op jit(solution)/shard_map/reduce_scatter | solution.py:212
  683.3 200.7 %reduce-scatter.7.cloned.1.call-start = ((), (), s32[]{:S(2)}) async-start(), calls=%async_computation.7 | async-start | bytes 15728640 | tf_op jit(solution)/shard_map/reduce_scatter | solution.py:181
  706.1 82.2 %copy-start.31 = (f32[3,512]{1,0:T(4,128)S(1)}, f32[3,512]{1,0:T(4,128)}, u32[]{:S(2)}) copy-start(f32[3,512]{1,0:T(4,128)} %copy-done.30) | copy-start | bytes 18436
  706.1 82.2 %copy-start.27 = (f32[3,512]{1,0:T(4,128)S(1)}, f32[3,512]{1,0:T(4,128)}, u32[]{:S(2)}) copy-start(f32[3,512]{1,0:T(4,128)} %copy-done.26) | copy-start | bytes 18436
  706.2 275.4 %all-gather.11.cloned.1.call-start = ((), (), s32[]{:S(2)}) async-start(), calls=%async_computation.10 | async-start | bytes 15728640 | tf_op jit(solution)/shard_map/all_gather | solution.py:220
  788.4 95.6 %copy-start.42 = (f32[1024]{0:T(1024)S(1)}, f32[1024]{0:T(1024)}, u32[]{:S(2)}) copy-start(f32[1024]{0:T(1024)} %param.37) | copy-start | bytes 12292
  788.4 95.6 %copy-start.44 = (f32[3]{0:T(128)S(1)}, f32[3]{0:T(128)}, u32[]{:S(2)}) copy-start(f32[3]{0:T(128)} %copy-done.43) | copy-start | bytes 40
  899.2 902.9 %all-reduce.5.cloned.1.call-start = ((), (), s32[]{:S(2)}) async-start(), calls=%async_computation.12 | async-start | bytes 12582912 | tf_op jit(solution)/shard_map/psum | solution.py:268
  918.9 62.7 %copy-start.19 = (bf16[256,1024]{1,0:T(8,128)(2,1)S(1)}, bf16[256,1024]{1,0:T(8,128)(2,1)}, u32[]{:S(2)}) copy-start(bf16[256,1024]{1,0:T(8,128)(2,1)} %param.32) | copy-start | bytes 1572868
  1028.9 17.5 copy-start.6
  1068.4 17.5 copy-start.6
  1098.5 9.4 copy-start.4
  1108.0 17.5 copy-start.6
  1138.1 9.4 copy-start.4
  1147.5 17.5 copy-start.6
  1213.3 17.5 copy-start.6
  1243.4 9.4 copy-start.4
  1252.9 17.5 copy-start.6
  1292.4 17.5 copy-start.6
  1322.5 9.4 copy-start.4
  1332.0 17.5 copy-start.6
  1397.8 17.5 copy-start.6
  1437.3 17.5 copy-start.6
  1476.9 17.5 copy-start.6
  1516.4 17.5 copy-start.6
  1563.5 9.9 copy-start.15
  1563.5 9.9 copy-start.16
  1563.5 9.9 copy-start.17
  1587.3 315.7 %reduce-scatter.11.cloned.1.call-start = ((), (), s32[]{:S(2)}) async-start(), calls=%async_computation.11 | async-start | bytes 15728640 | tf_op jit(solution)/shard_map/reduce_scatter | solution.py:261
  1806.4 11.7 copy-start.18
  1812.1 90.8 %copy-start.22 = (f32[3,512]{1,0:T(4,128)S(1)}, f32[3,512]{1,0:T(4,128)}, u32[]{:S(2)}) copy-start(f32[3,512]{1,0:T(4,128)} %copy-done.21) | copy-start | bytes 18436
  1812.1 90.8 %copy-start.34 = (f32[1024]{0:T(1024)S(1)}, f32[1024]{0:T(1024)}, u32[]{:S(2)}) copy-start(f32[1024]{0:T(1024)} %param.38) | copy-start | bytes 12292
  1818.0 89.3 %copy-start.29 = (f32[3,512]{1,0:T(4,128)S(1)}, f32[3,512]{1,0:T(4,128)}, u32[]{:S(2)}) copy-start(f32[3,512]{1,0:T(4,128)} %copy-done.28) | copy-start | bytes 18436
  1818.0 89.4 %copy-start.25 = (f32[3,512]{1,0:T(4,128)S(1)}, f32[3,512]{1,0:T(4,128)}, u32[]{:S(2)}) copy-start(f32[3,512]{1,0:T(4,128)} %copy-done.24) | copy-start | bytes 18436
  1821.7 91.2 %copy-start.35 = (f32[1024]{0:T(1024)S(1)}, f32[1024]{0:T(1024)}, u32[]{:S(2)}) copy-start(f32[1024]{0:T(1024)} %get-tuple-element.318) | copy-start | bytes 12292
  1821.7 91.2 %copy-start.36 = (f32[1024]{0:T(1024)S(1)}, f32[1024]{0:T(1024)}, u32[]{:S(2)}) copy-start(f32[1024]{0:T(1024)} %get-tuple-element.314) | copy-start | bytes 12292
  1821.7 91.2 %copy-start.37 = (f32[1024]{0:T(1024)S(1)}, f32[1024]{0:T(1024)}, u32[]{:S(2)}) copy-start(f32[1024]{0:T(1024)} %get-tuple-element.396) | copy-start | bytes 12292
  1821.7 91.2 %copy-start.38 = (f32[1024]{0:T(1024)S(1)}, f32[1024]{0:T(1024)}, u32[]{:S(2)}) copy-start(f32[1024]{0:T(1024)} %get-tuple-element.411) | copy-start | bytes 12292
  (81 other events, 368.2 us)
Sparse Core Ops, SparseCore 0:
  16.5 84.7 all-gather.4
  347.2 99.0 reduce-scatter.4
  456.9 82.0 all-gather.6
  540.5 82.0 all-gather.8
  683.4 99.0 reduce-scatter.8
  785.0 99.0 reduce-scatter.6
  899.4 82.1 all-gather.10
  1587.4 214.7 all-reduce.4
  1804.9 97.9 reduce-scatter.10
where the time goes:
time: 1990 us; the launch traced here: 1970 us
  waiting for transfers between devices  715 us (36%)
  matrix products  649 us (33%)
  other arithmetic  334 us (17%)
  local copies, waits for them, and re-layouts  196 us (10%)
  blocking collectives  62.6 us (3%)
    psum x1, waiting for transfers between devices, shards(): lax.psum(query_key_value_gradient.astype(jnp.bfloat16), 'dp')  168 us
    convert_element_type x12, other arithmetic, one_block(): grad_low = grad_scores.astype(jnp.bfloat16)  127 us
    dot_general x12, matrix products, one_block(): jnp.einsum('qhd,khd->hqk', grad_block, values, preferred_element_type=jnp...  113 us
    reduce_scatter x1, waiting for transfers between devices, shards(): lax.psum_scatter(attn_part.astype(jnp.bfloat16), 'tensor', scatter_dimens...  99.1 us
    reduce_scatter x1, waiting for transfers between devices, shards(): lax.psum_scatter(perceptron_portion.astype(jnp.bfloat16), 'tensor', scatt...  88.3 us
    all_gather x1, waiting for transfers between devices, shards(): normalized_every = lax.all_gather(normed, 'tensor', axis=1, tiled=True)  84.7 us
    dot_general x12, matrix products, one_block(): jnp.einsum('hqk,khd->qhd', grad_low, key_rows, preferred_element_type=jnp...  82.8 us
    dot_general x24, matrix products, one_block(): jnp.einsum('qhd,khd->hqk', query_block, key_rows, preferred_element_type=...  82.5 us
  transfers between devices with their start and end apart: 9, of which 8 were waited for; matrix products, arithmetic and copies ran while one was open for 11% of the time, Pallas kernels for 0%

commit v1 on v0

--- a/solution.py
+++ b/solution.py
@@ -272,7 +272,13 @@
         lax.psum(grad_up_bias.astype(jnp.bfloat16), "dp").astype(jnp.float32),
         lax.psum(down_gradient.astype(jnp.bfloat16), "dp").astype(jnp.float32),
     )
-    small_sums = lax.psum(
+
+    def lift_the_widths(shard_axis, peer_axis, vec):
+        return jax.lax.psum(jax.lax.psum(vec, shard_axis), peer_axis)
+
+    small_sums = lift_the_widths(
+        "tensor",
+        "dp",
         (
             grad_attn_gain,
             grad_attn_shift,
@@ -281,7 +287,6 @@
             grad_out_bias,
             grad_down_bias,
         ),
-        ("dp", "tensor"),
     )
     return (
         output,

time: 1990 us -> 1990 us (level)
    psum x1 -> x2, blocking collectives: 39.7 us -> 47.4 us  [lift_the_widths(): return jax.lax.psum(jax.lax.psum(vec, shard_axis), peer_axis)]
where the time goes in v1:
time: 1990 us; the launch traced here: 1980 us
  waiting for transfers between devices  715 us (36%)
  matrix products  647 us (33%)
  other arithmetic  335 us (17%)
  local copies, waits for them, and re-layouts  196 us (10%)
  blocking collectives  70.3 us (4%)
    psum x1, waiting for transfers between devices, shards(): lax.psum(query_key_value_gradient.astype(jnp.bfloat16), 'dp')  168 us
    convert_element_type x12, other arithmetic, one_block(): grad_low = grad_scores.astype(jnp.bfloat16)  127 us
    dot_general x12, matrix products, one_block(): jnp.einsum('qhd,khd->hqk', grad_block, values, preferred_element_type=jnp...  111 us
    reduce_scatter x1, waiting for transfers between devices, shards(): lax.psum_scatter(attn_part.astype(jnp.bfloat16), 'tensor', scatter_dimens...  99.2 us
    reduce_scatter x1, waiting for transfers between devices, shards(): lax.psum_scatter(perceptron_portion.astype(jnp.bfloat16), 'tensor', scatt...  88.3 us
    all_gather x1, waiting for transfers between devices, shards(): normalized_every = lax.all_gather(normed, 'tensor', axis=1, tiled=True)  84.7 us
    dot_general x12, matrix products, one_block(): jnp.einsum('hqk,khd->qhd', grad_low, key_rows, preferred_element_type=jnp...  82.8 us
    dot_general x24, matrix products, one_block(): jnp.einsum('qhd,khd->hqk', query_block, key_rows, preferred_element_type=...  82.5 us
  transfers between devices with their start and end apart: 9, of which 8 were waited for; matrix products, arithmetic and copies ran while one was open for 11% of the time, Pallas kernels for 0%

profile of v1, /device:TPU:0, one launch (start us, length us, event | category | flops | bytes accessed | tf_op | source)
XLA Modules:
  0.0 1979.8 jit_solution(14099493927202814894)
XLA Ops:
  16.7 84.7 %all-gather.5.cloned.1.call-done = bf16[3,2048,1024]{2,1,0:T(8,128)(2,1)} async-done(((bf16[3,512,1024]{2,1,0:T(8,128)(2,1)}), bf16[3,2048,1024]{2,1,0:T(8,128)(2,1)}) %all-gather.5.cloned.1.call-update) | async-done | bytes 12582928 | tf_op jit(solution)/shard_map/all_gather | solution.py:136
  101.4 17.0 fusion.58
  123.3 11.4 fusion.102
  134.7 9.3 add_convert_fusion.3
  144.0 192.8 %while.54 = (s32[]{:T(128)}, bf16[3,2048,4,64]{1,3,2,0:T(8,128)(2,1)}, f32[3,4,4,512]{3,2,1,0:T(4,128)}, bf16[3,2048,4,64]{1,3,2,0:T(8,128)(2,1)}, bf16[3,2048,4...) while((s32[]{:T(128)}, ...), condition=%wide.region_7.8_spmd, body=%wide.region_2.7_spmd.sunk | while | flops 1111619584 | bytes 74055984 | solution.py:148
  152.3 47.4 %while.57 = (s32[]{:T(128)}, bf16[4,512,4,64]{1,3,2,0:T(8,128)(2,1)}, f32[4,4,512]{2,1,0:T(4,128)S(1)}, bf16[4,512,4,64]{1,3,2,0:T(8,128)(2,1)}, bf16[2048,4,64]...) while((s32[]{:T(128)}, bf16[4,512,4,64]{1,3,2,0:T(8,128)(2,1)}, ...), condition=%wide.region_6.6_spmd, body=%wide.region_3.5_spmd.sunk | while | flops 1111619584 | bytes 57213052 | solution.py:46
  216.5 47.4 %while.57 = (s32[]{:T(128)}, bf16[4,512,4,64]{1,3,2,0:T(8,128)(2,1)}, f32[4,4,512]{2,1,0:T(4,128)S(1)}, bf16[4,512,4,64]{1,3,2,0:T(8,128)(2,1)}, bf16[2048,4,64]...) while((s32[]{:T(128)}, bf16[4,512,4,64]{1,3,2,0:T(8,128)(2,1)}, ...), condition=%wide.region_6.6_spmd, body=%wide.region_3.5_spmd.sunk | while | flops 1111619584 | bytes 57213052 | solution.py:46
  280.7 47.4 %while.57 = (s32[]{:T(128)}, bf16[4,512,4,64]{1,3,2,0:T(8,128)(2,1)}, f32[4,4,512]{2,1,0:T(4,128)S(1)}, bf16[4,512,4,64]{1,3,2,0:T(8,128)(2,1)}, bf16[2048,4,64]...) while((s32[]{:T(128)}, bf16[4,512,4,64]{1,3,2,0:T(8,128)(2,1)}, ...), condition=%wide.region_6.6_spmd, body=%wide.region_3.5_spmd.sunk | while | flops 1111619584 | bytes 57213052 | solution.py:46
  336.8 10.1 convolution_convert_fusion.2
  347.0 99.2 %reduce-scatter.5.cloned.1.call-done = bf16[3,512,1024]{2,1,0:T(8,128)(2,1)} async-done(((bf16[3,2048,1024]{2,1,0:T(8,128)(2,1)}), bf16[3,512,1024]{2,1,0:T(8,128)(2,1)}) %reduce-scatter.5.cloned.1.call-update) | async-done | bytes 3145744 | tf_op jit(solution)/shard_map/reduce_scatter | solution.py:156
  465.1 73.8 %all-gather.7.cloned.1.call-done = bf16[3,2048,1024]{2,1,0:T(8,128)(2,1)} async-done(((bf16[3,512,1024]{2,1,0:T(8,128)(2,1)}), bf16[3,2048,1024]{2,1,0:T(8,128)(2,1)}) %all-gather.7.cloned.1.call-update) | async-done | bytes 12582928 | tf_op jit(solution)/shard_map/all_gather | solution.py:163
  539.0 29.6 %fusion.72 = (u8[2048,1024]{1,0:T(8,128)(4,1)}, u8[2048,1024]{1,0:T(8,128)(4,1)}, f32[3,2048,1024]{2,1,0:T(8,128)}) fusion(f32[1024]{0:T(1024)S(1)} %copy-done.41, bf16[3,2048,1024]{2,1,0:T(8,128)(2,1)} %all-gather.7.cloned.1.call-done, bf16[1024,1024]{1,0:T(8,128)(2,1)S(1)} %copy-done), kind=kOutput, calls=%fused_computation.128 | convolution fusion | flops 12968787968 | bytes 44044288 | tf_op jit(solution)/shard_map/jzb,bu->jzu/dot_general | solution.py:165
  568.6 61.5 %multiply_convert_fusion.1 = (bf16[3,2048,1024]{2,1,0:T(8,128)(2,1)}, f32[3,2048,1024]{2,1,0:T(8,128)}) fusion(f32[3,2048,1024]{2,1,0:T(8,128)} %get-tuple-element.418, f32[1024]{0:T(1024)S(1)} %copy-done.41, u8[2048,1024]{1,0:T(8,128)(4,1)} %get-tuple-element.313, u8[2048,1024]{1,0:T(8,128)(4,1)} %get-tuple-element.312), kind=kLoop, calls=%fused_computation.67 | loop fusion | flops 446693376 | bytes 67112960 | tf_op jit(solution)/shard_map/convert_element_type | solution.py:174
  630.1 32.6 %fusion.103 = (bf16[1024]{0:T(1024)(128)(2,1)}, bf16[3,2048,1024]{2,1,0:T(8,128)(2,1)}) fusion(f32[3,2048,1024]{2,1,0:T(8,128)} %get-tuple-element.405, bf16[3,2048,1024]{2,1,0:T(8,128)(2,1)} %all-gather.9.cloned.1.call-done, bf16[1024,1024]{1,0:T(8,128)(2,1)} %param.36, f32[3,2048,1024]{2,1,0:T(8,128)} %get-tuple-element.418, f32[1024]{0:T(1024)S(1)} %copy-done.41), kind=kOutput, calls=%fused_computation.192 | convolution fusion | flops 12985564160 | bytes 77600768 | tf_op jit(solution)/shard_map/eph,wh->epw/dot_general | solution.py:186
  662.7 20.3 %convolution_convert_fusion = bf16[3,2048,1024]{2,1,0:T(8,128)(2,1)} fusion(bf16[3,2048,1024]{2,1,0:T(8,128)(2,1)} %get-tuple-element.420, bf16[1024,1024]{1,0:T(8,128)(2,1)S(1)} %copy-done), kind=kOutput, calls=%fused_computation.105 | convolution fusion | flops 12891193344 | bytes 27262976 | tf_op jit(solution)/shard_map/jmn,hn->jmh/dot_general | solution.py:206
  684.6 21.2 %convolution_convert_fusion.1 = bf16[3,2048,1024]{2,1,0:T(8,128)(2,1)} fusion(bf16[3,2048,1024]{2,1,0:T(8,128)(2,1)} %get-tuple-element.404, bf16[1024,1024]{1,0:T(8,128)(2,1)S(1)} %copy-done.47), kind=kOutput, calls=%fused_computation.106 | convolution fusion | flops 12891193344 | bytes 27262976 | tf_op jit(solution)/shard_map/vuc,cy->vuy/dot_general | solution.py:175
  706.1 76.2 %reduce-scatter.9.cloned.1.call-done = bf16[3,512,1024]{2,1,0:T(8,128)(2,1)} async-done(((bf16[3,2048,1024]{2,1,0:T(8,128)(2,1)}), bf16[3,512,1024]{2,1,0:T(8,128)(2,1)}) %reduce-scatter.9.cloned.1.call-update) | async-done | bytes 3145744 | tf_op jit(solution)/shard_map/reduce_scatter | solution.py:212
  795.4 88.3 %reduce-scatter.7.cloned.1.call-done = bf16[3,512,1024]{2,1,0:T(8,128)(2,1)} async-done(((bf16[3,2048,1024]{2,1,0:T(8,128)(2,1)}), bf16[3,512,1024]{2,1,0:T(8,128)(2,1)}) %reduce-scatter.7.cloned.1.call-update) | async-done | bytes 3145744 | tf_op jit(solution)/shard_map/reduce_scatter | solution.py:181
  883.8 10.3 fusion.100
  899.1 19.5 bitcast_convert_fusion.1
  918.6 19.0 bitcast_convert_fusion.2
  937.6 43.7 %all-gather.11.cloned.1.call-done = bf16[3,2048,1024]{2,1,0:T(8,128)(2,1)} async-done(((bf16[3,512,1024]{2,1,0:T(8,128)(2,1)}), bf16[3,2048,1024]{2,1,0:T(8,128)(2,1)}) %all-gather.11.cloned.1.call-update) | async-done | bytes 12582928 | tf_op jit(solution)/shard_map/all_gather | solution.py:220
  981.3 14.3 convolution_convert_fusion.3
  995.6 551.7 %while.56 = (s32[]{:T(128)}, bf16[3,2048,4,64]{1,3,2,0:T(8,128)(2,1)}, bf16[3,2048,4,64]{1,3,2,0:T(8,128)(2,1)}, bf16[3,2048,4,64]{1,3,2,0:T(8,128)(2,1)}, bf16[...) while((s32[]{:T(128)}, ...), condition=%wide.region_22.23_spmd, body=%wide.region_18.22_spmd.sunk | while | flops 2737436672 | bytes 246014544 | solution.py:235
  1010.5 157.5 %while.58 = (s32[]{:T(128)}, f32[2048,4,64]{0,2,1:T(8,128)}, f32[2048,4,64]{0,2,1:T(8,128)}, bf16[4,512,4,64]{1,3,2,0:T(8,128)(2,1)}, bf16[4,512,4,64]{1,3,2,0:T...) while((s32[]{:T(128)}, f32[2048,4,64]{0,2,1:T(8,128)}, ...), condition=%wide.region_21.21_spmd.clone, body=%wide.region_19.20_spmd.clone.sunk | while | flops 2737436672 | bytes 206102832 | solution.py:90
  1028.4 10.5 multiply_convert_fusion.4
  1067.8 10.5 multiply_convert_fusion.4
  1107.2 10.5 multiply_convert_fusion.4
  1146.6 10.5 multiply_convert_fusion.4
  1194.3 157.5 %while.58 = (s32[]{:T(128)}, f32[2048,4,64]{0,2,1:T(8,128)}, f32[2048,4,64]{0,2,1:T(8,128)}, bf16[4,512,4,64]{1,3,2,0:T(8,128)(2,1)}, bf16[4,512,4,64]{1,3,2,0:T...) while((s32[]{:T(128)}, f32[2048,4,64]{0,2,1:T(8,128)}, ...), condition=%wide.region_21.21_spmd.clone, body=%wide.region_19.20_spmd.clone.sunk | while | flops 2737436672 | bytes 206102832 | solution.py:90
  1202.9 9.2 multiply_reduce_fusion.5
  1212.2 10.5 multiply_convert_fusion.4
  1251.6 10.5 multiply_convert_fusion.4
  1290.9 10.5 multiply_convert_fusion.4
  1330.3 10.5 multiply_convert_fusion.4
  1378.1 157.5 %while.58 = (s32[]{:T(128)}, f32[2048,4,64]{0,2,1:T(8,128)}, f32[2048,4,64]{0,2,1:T(8,128)}, bf16[4,512,4,64]{1,3,2,0:T(8,128)(2,1)}, bf16[4,512,4,64]{1,3,2,0:T...) while((s32[]{:T(128)}, f32[2048,4,64]{0,2,1:T(8,128)}, ...), condition=%wide.region_21.21_spmd.clone, body=%wide.region_19.20_spmd.clone.sunk | while | flops 2737436672 | bytes 206102832 | solution.py:90
  1396.0 10.5 multiply_convert_fusion.4
  1435.4 10.5 multiply_convert_fusion.4
  1474.8 10.5 multiply_convert_fusion.4
  1514.1 10.5 multiply_convert_fusion.4
  1561.1 9.9 fusion.89
  1571.0 13.9 fusion.86
  1586.3 15.4 bitcast_convert_fusion
  1606.8 22.8 %all-reduce.2 = (bf16[2,256]{1,0:T(2,128)(2,1)S(1)}, bf16[1024]{0:T(1024)(128)(2,1)S(1)}) all-reduce(bf16[2,256]{1,0:T(2,128)(2,1)S(1)} %pad_maximum_fusion.7, bf16[1024]{0:T(1024)(128)(2,1)S(1)} %copy-done.45), channel_id=1, replica_groups=mesh['dp'=8,'tensor'=4] {'dp'}, use_global_device_ids=true, to_apply=%region_29.30 | all-reduce | flops 1536 | bytes 6144 | tf_op jit(solution)/shard_map/psum | solution.py:269
  1632.2 167.6 %all-reduce.6.cloned.1.call-done = (bf16[3,1024,256]{1,2,0:T(8,128)(2,1)}, bf16[256,1024]{1,0:T(8,128)(2,1)}, bf16[1024,1024]{1,0:T(8,128)(2,1)}, bf16[1024,1024]{1,0:T(8,128)(2,1)}) async-done(((bf16[3,1024,256]{1,2,0:T(8,128)(2,1)}, bf16[256,1024]{1,0:T(8,128)(2,1)}, bf16[1024,1024]{1,0:T(8,128)(2,1)}, bf16[1024,1024]{1,0:T(8,128)(2,1)}), (bf16[3,1024,256]{1,2,0:T(8,128)(2,1)}, ...) | async-done | bytes 6291472 | tf_op jit(solution)/shard_map/psum | solution.py:268
  1819.5 81.1 %reduce-scatter.11.cloned.1.call-done = bf16[3,512,1024]{2,1,0:T(8,128)(2,1)} async-done(((bf16[3,2048,1024]{2,1,0:T(8,128)(2,1)}), bf16[3,512,1024]{2,1,0:T(8,128)(2,1)}) %reduce-scatter.11.cloned.1.call-update) | async-done | bytes 3145744 | tf_op jit(solution)/shard_map/reduce_scatter | solution.py:261
  1910.6 10.3 all-reduce.1
  1920.8 37.2 %all-reduce = (f32[1024]{0:T(1024)S(1)}, f32[1024]{0:T(1024)S(1)}, f32[1024]{0:T(1024)S(1)}, f32[1024]{0:T(1024)S(1)}, f32[1024]{0:T(1024)S(1)}, /*index=5*/f32[1024]{0:T(1024)S(1)}) all-reduce(f32[1024]{0:T(1024)S(1)} %get-tuple-element.390, f32[1024]{0:T(1024)S(1)} %get-tuple-element.391, ...), channel_id=1, replica_groups=mesh['dp'=8,'tensor'=4] {'dp'}, use_global_device_ids=true, to_apply=%region_33.34 | all-reduce | flops 6144 | bytes 49152 | tf_op jit(solution)/shard_map/psum | solution.py:277
  (519 shorter events, 727.3 us)
Async XLA Ops:
  7.2 531.8 %copy-start = (bf16[1024,1024]{1,0:T(8,128)(2,1)S(1)}, bf16[1024,1024]{1,0:T(8,128)(2,1)}, u32[]{:S(2)}) copy-start(bf16[1024,1024]{1,0:T(8,128)(2,1)} %param.34) | copy-start | bytes 6291460
  7.2 94.1 %all-gather.5.cloned.1.call-start = ((), (), s32[]{:S(2)}) async-start(), calls=%async_computation.4 | async-start | bytes 15728640 | tf_op jit(solution)/shard_map/all_gather | solution.py:136
  16.4 429.7 %reduce-scatter.5.cloned.1.call-start = ((), (), s32[]{:S(2)}) async-start(), calls=%async_computation.5 | async-start | bytes 15728640 | tf_op jit(solution)/shard_map/reduce_scatter | solution.py:156
  346.9 99.3 %copy-start.23 = (f32[1024]{0:T(1024)S(1)}, f32[1024]{0:T(1024)}, u32[]{:S(2)}) copy-start(f32[1024]{0:T(1024)} %param.33) | copy-start | bytes 12292
  346.9 106.8 %copy-start.32 = (f32[1024]{0:T(1024)S(1)}, f32[1024]{0:T(1024)}, u32[]{:S(2)}) copy-start(f32[1024]{0:T(1024)} %param.40) | copy-start | bytes 12292
  346.9 106.7 %copy-start.39 = (f32[1024]{0:T(1024)S(1)}, f32[1024]{0:T(1024)}, u32[]{:S(2)}) copy-start(f32[1024]{0:T(1024)} %param.41) | copy-start | bytes 12292
  346.9 192.0 %all-gather.7.cloned.1.call-start = ((), (), s32[]{:S(2)}) async-start(), calls=%async_computation.6 | async-start | bytes 15728640 | tf_op jit(solution)/shard_map/all_gather | solution.py:163
  456.7 82.3 %copy-start.41 = (f32[1024]{0:T(1024)S(1)}, f32[1024]{0:T(1024)}, u32[]{:S(2)}) copy-start(f32[1024]{0:T(1024)} %param.35) | copy-start | bytes 12292
  456.7 173.4 %all-gather.9.cloned.1.call-start = ((), (), s32[]{:S(2)}) async-start(), calls=%async_computation.8 | async-start | bytes 15728640 | tf_op jit(solution)/shard_map/all_gather | solution.py:185
  460.3 108.3 %copy-start.43 = (f32[3]{0:T(128)}, f32[3]{0:T(128)S(1)}, u32[]{:S(2)}) copy-start(f32[3]{0:T(128)S(1)} %dynamic_slice.47) | copy-start | bytes 40
  465.1 317.2 %reduce-scatter.9.cloned.1.call-start = ((), (), s32[]{:S(2)}) async-start(), calls=%async_computation.9 | async-start | bytes 15728640 | tf_op jit(solution)/shard_map/reduce_scatter | solution.py:212
  683.1 200.7 %reduce-scatter.7.cloned.1.call-start = ((), (), s32[]{:S(2)}) async-start(), calls=%async_computation.7 | async-start | bytes 15728640 | tf_op jit(solution)/shard_map/reduce_scatter | solution.py:181
  705.9 82.2 %copy-start.31 = (f32[3,512]{1,0:T(4,128)S(1)}, f32[3,512]{1,0:T(4,128)}, u32[]{:S(2)}) copy-start(f32[3,512]{1,0:T(4,128)} %copy-done.30) | copy-start | bytes 18436
  705.9 82.2 %copy-start.27 = (f32[3,512]{1,0:T(4,128)S(1)}, f32[3,512]{1,0:T(4,128)}, u32[]{:S(2)}) copy-start(f32[3,512]{1,0:T(4,128)} %copy-done.26) | copy-start | bytes 18436
  705.9 275.4 %all-gather.11.cloned.1.call-start = ((), (), s32[]{:S(2)}) async-start(), calls=%async_computation.10 | async-start | bytes 15728640 | tf_op jit(solution)/shard_map/all_gather | solution.py:220
  788.1 95.7 %copy-start.42 = (f32[1024]{0:T(1024)S(1)}, f32[1024]{0:T(1024)}, u32[]{:S(2)}) copy-start(f32[1024]{0:T(1024)} %param.37) | copy-start | bytes 12292
  788.1 95.7 %copy-start.44 = (f32[3]{0:T(128)S(1)}, f32[3]{0:T(128)}, u32[]{:S(2)}) copy-start(f32[3]{0:T(128)} %copy-done.43) | copy-start | bytes 40
  899.0 900.8 %all-reduce.6.cloned.1.call-start = ((), (), s32[]{:S(2)}) async-start(), calls=%async_computation.12 | async-start | bytes 12582912 | tf_op jit(solution)/shard_map/psum | solution.py:268
  918.6 62.7 %copy-start.19 = (bf16[256,1024]{1,0:T(8,128)(2,1)S(1)}, bf16[256,1024]{1,0:T(8,128)(2,1)}, u32[]{:S(2)}) copy-start(bf16[256,1024]{1,0:T(8,128)(2,1)} %param.32) | copy-start | bytes 1572868
  1028.4 17.5 copy-start.6
  1067.8 17.5 copy-start.6
  1107.2 17.5 copy-start.6
  1146.6 17.5 copy-start.6
  1202.9 9.3 copy-start.4
  1212.2 17.5 copy-start.6
  1251.6 17.5 copy-start.6
  1281.7 9.3 copy-start.4
  1290.9 17.5 copy-start.6
  1321.1 9.3 copy-start.4
  1330.3 17.5 copy-start.6
  1396.0 17.5 copy-start.6
  1426.1 9.3 copy-start.4
  1435.4 17.5 copy-start.6
  1474.8 17.5 copy-start.6
  1514.1 17.5 copy-start.6
  1561.1 9.9 copy-start.15
  1561.1 9.9 copy-start.16
  1561.1 9.9 copy-start.17
  1584.9 315.7 %reduce-scatter.11.cloned.1.call-start = ((), (), s32[]{:S(2)}) async-start(), calls=%async_computation.11 | async-start | bytes 15728640 | tf_op jit(solution)/shard_map/reduce_scatter | solution.py:261
  1804.1 11.8 copy-start.18
  1809.8 90.8 %copy-start.22 = (f32[3,512]{1,0:T(4,128)S(1)}, f32[3,512]{1,0:T(4,128)}, u32[]{:S(2)}) copy-start(f32[3,512]{1,0:T(4,128)} %copy-done.21) | copy-start | bytes 18436
  1809.8 90.8 %copy-start.34 = (f32[1024]{0:T(1024)S(1)}, f32[1024]{0:T(1024)}, u32[]{:S(2)}) copy-start(f32[1024]{0:T(1024)} %param.38) | copy-start | bytes 12292
  1815.9 89.2 %copy-start.29 = (f32[3,512]{1,0:T(4,128)S(1)}, f32[3,512]{1,0:T(4,128)}, u32[]{:S(2)}) copy-start(f32[3,512]{1,0:T(4,128)} %copy-done.28) | copy-start | bytes 18436
  1815.9 89.2 %copy-start.25 = (f32[3,512]{1,0:T(4,128)S(1)}, f32[3,512]{1,0:T(4,128)}, u32[]{:S(2)}) copy-start(f32[3,512]{1,0:T(4,128)} %copy-done.24) | copy-start | bytes 18436
  1819.5 91.1 %copy-start.35 = (f32[1024]{0:T(1024)S(1)}, f32[1024]{0:T(1024)}, u32[]{:S(2)}) copy-start(f32[1024]{0:T(1024)} %get-tuple-element.318) | copy-start | bytes 12292
  1819.5 91.1 %copy-start.36 = (f32[1024]{0:T(1024)S(1)}, f32[1024]{0:T(1024)}, u32[]{:S(2)}) copy-start(f32[1024]{0:T(1024)} %get-tuple-element.314) | copy-start | bytes 12292
  1819.5 91.1 %copy-start.37 = (f32[1024]{0:T(1024)S(1)}, f32[1024]{0:T(1024)}, u32[]{:S(2)}) copy-start(f32[1024]{0:T(1024)} %get-tuple-element.402) | copy-start | bytes 12292
  1819.5 91.1 %copy-start.38 = (f32[1024]{0:T(1024)S(1)}, f32[1024]{0:T(1024)}, u32[]{:S(2)}) copy-start(f32[1024]{0:T(1024)} %get-tuple-element.417) | copy-start | bytes 12292
  (81 other events, 367.1 us)
Sparse Core Ops, SparseCore 0:
  16.5 84.7 all-gather.4
  347.0 99.0 reduce-scatter.4
  456.8 82.0 all-gather.6
  540.4 82.0 all-gather.8
  683.2 99.0 reduce-scatter.8
  784.7 99.0 reduce-scatter.6
  899.1 82.0 all-gather.10
  1585.1 214.7 all-reduce.5
  1802.6 97.9 reduce-scatter.10
